TPU v7x, 1024 devices: a whole 4x8x16 slice. The times are simulated.
1024 devices in a mesh: ctx: 64 (over x, y, z_hi), tp: 16 (over z_lo, core).
Axes of the slice: x: 4, y: 8, z: 16 (z_hi: 2, z_lo: 8; z = z_hi * 8 + z_lo), core: 2. Of those that a mesh axis runs over, the one named last changes fastest.
Arguments:
- streams: bfloat16 [3, 4096, 8192], P(None, 'tp', 'ctx'), may hold values from -6 to 6
- medium_taps: float32 [4096, 128], P('tp'), may hold values from -0.5 to 0.5
- decay_rates: float32 [4096, 16], P('tp'), may hold values from 5e-06 to 0.1
- mode_weights: float32 [4096, 16], P('tp'), may hold values from -1.5 to 1.5
- skip_gain: float32 [4096], P('tp'), may hold values from -1 to 1
Outputs:
- gated_output: bfloat16 [4096, 8192], P('tp', 'ctx')
All inputs are finite; a program needn't handle non-finite values.
Results may differ from a plain program's by a relative error of at most 0.01.
Values may be sent and summed in bfloat16 or wider, within the bound.
A program may use at most 32 MiB of HBM per device.

v0:
```python
import functools

import jax
import jax.numpy as jnp
from jax import lax
from jax.experimental import pallas as pl
from jax.experimental.pallas import tpu as pltpu
from jax.sharding import PartitionSpec as P

MESH = pl.DeviceIdType.MESH
F32 = jnp.float32
BF16 = jnp.bfloat16
X, Y, Z = 4, 8, 16
LANES = 128
CHUNK = 128
TAPS = 128
MODES = 16
SUBS = 8
STEP = CHUNK // SUBS
GROUPS = 2


def place():
    ctx = lax.axis_index("ctx")
    return ctx, lax.axis_index("tp"), ctx // 16, (ctx // 2) % 8, ctx % 2


def ctx_of(x, y, hi):
    return (lax.rem(x + X, X) * Y + lax.rem(y + Y, Y)) * 2 + hi


def kernel(
    streams, taps, rates, weights, skip, out,
    vbuf, kbuf, qbuf, traw, rraw, wraw, sraw, halo,
    xw, kw, tapsT, coef, rows, gated, local, carry, mixed,
    ybuf, xbuf, zbuf, in_sem, send_sem, halo_sem, y_sem, x_sem, z_sem,
):
    ctx, tp, x, y, hi = place()
    count = lax.axis_size("ctx")
    loads = []
    for n, (src, dst) in enumerate(
        ((rates, rraw), (weights, wraw), (taps, traw), (streams.at[2], vbuf),
         (streams.at[1], kbuf), (skip, sraw), (streams.at[0], qbuf))
    ):
        copy = pltpu.make_async_copy(src, dst, in_sem.at[n])
        copy.start()
        loads.append(copy)

    after = lax.rem(ctx + 1, count)
    before = lax.rem(ctx + count - 1, count)
    mate = ctx + 1 - 2 * hi
    partners = [after, before]
    partners += [ctx_of(x, y + d, hi) for d in range(1, Y)]
    partners += [ctx_of(x + d, y, hi) for d in range(1, X)]
    barrier = pltpu.get_barrier_semaphore()
    for p in partners:
        pl.semaphore_signal(barrier, inc=1, device_id=(p, tp), device_id_type=MESH)

    loads[0].wait()
    loads[1].wait()
    sub = lax.broadcasted_iota(jnp.int32, (SUBS, LANES), 0)
    subf = sub.astype(F32)
    yf = y.astype(F32)
    for g in range(GROUPS):
        part = pl.ds(g * LANES, LANES)
        rate = rraw[part, :].T
        weight = wraw[part, :].T
        rows[g, 0] = jnp.exp(-rate)
        rows[g, 1] = weight * jnp.sqrt(2.0 * rate)
        rows[g, 2] = jnp.exp(-128.0 * rate)
        rows[g, 3] = jnp.exp(-256.0 * rate)
        rows[g, 4] = jnp.exp(-2048.0 * rate)
        rows[g, 5] = jnp.exp((-256.0 * yf) * rate)
        rows[g, 6] = rate
        for r in range(MODES):
            lam = jnp.broadcast_to(rows[g, 6, r : r + 1, :], (SUBS, LANES))
            coef[g, r, 0] = jnp.where(sub >= 1, jnp.exp(-16.0 * lam), 0.0)
            coef[g, r, 1] = jnp.where(sub >= 2, jnp.exp(-32.0 * lam), 0.0)
            coef[g, r, 2] = jnp.where(sub >= 4, jnp.exp(-64.0 * lam), 0.0)
            coef[g, r, 3] = jnp.exp(-16.0 * subf * lam)

    pl.semaphore_wait(barrier, len(partners))
    sends = []
    for g in range(GROUPS):
        copy = pltpu.make_async_remote_copy(
            src_ref=streams.at[2, pl.ds(g * LANES, LANES), :],
            dst_ref=halo.at[g],
            send_sem=send_sem.at[g],
            recv_sem=halo_sem.at[g],
            device_id=(after, tp),
            device_id_type=MESH,
        )
        copy.start()
        sends.append(copy)

    loads[2].wait()
    loads[3].wait()
    loads[4].wait()
    loads[5].wait()
    for g in range(GROUPS):
        part = pl.ds(g * LANES, LANES)
        tapsT[g] = traw[part, :].T
        xw[g, pl.ds(CHUNK, CHUNK), :] = vbuf[part, :].astype(F32).T
        kw[g] = kbuf[part, :].astype(F32).T

    def exchange(g, which, src, dst_of, sem, devices):
        for n, d in enumerate(devices):
            copy = pltpu.make_async_remote_copy(
                src_ref=src,
                dst_ref=dst_of(n),
                send_sem=send_sem.at[2 + g * 11 + which + n],
                recv_sem=sem.at[g, n],
                device_id=(d, tp),
                device_id_type=MESH,
            )
            copy.start()
            sends.append(copy)
            yield copy

    y_copies, x_copies, z_copies = {}, {}, {}
    for g in range(GROUPS):
        sends[g].wait_recv()
        past = halo[g].astype(F32).T
        xw[g, pl.ds(0, CHUNK), :] = jnp.where(ctx > 0, past, 0.0)

        def fir(block, acc):
            base = CHUNK - 8 * block
            tap = [
                jnp.broadcast_to(tapsT[g, pl.ds(8 * block + jj, 1), :], (SUBS, LANES))
                for jj in range(8)
            ]
            window = {
                m: xw[g, pl.ds(base + m, SUBS, stride=STEP), :] for m in range(-7, STEP)
            }
            acc = list(acc)
            for jj in range(8):
                for i in range(STEP):
                    acc[i] = acc[i] + tap[jj] * window[i - jj]
            return tuple(acc)

        zero = jnp.zeros((SUBS, LANES), F32)
        medium = lax.fori_loop(0, TAPS // 8, fir, (zero,) * STEP)
        gate = []
        for i in range(STEP):
            key = kw[g, pl.ds(i, SUBS, stride=STEP), :]
            value = (key * medium[i]).astype(BF16).astype(F32)
            gated[g, i] = value
            gate.append(value)
        for r in range(MODES):
            a = jnp.broadcast_to(rows[g, 0, r : r + 1, :], (SUBS, LANES))
            h = gate[0]
            for i in range(1, STEP):
                h = h * a + gate[i]
            h = h + coef[g, r, 0] * pltpu.roll(h, 1, 0)
            h = h + coef[g, r, 1] * pltpu.roll(h, 2, 0)
            h = h + coef[g, r, 2] * pltpu.roll(h, 4, 0)
            carry[g, r] = jnp.where(sub >= 1, pltpu.roll(h, 1, 0), 0.0)
            ybuf[g, 0, pl.ds(r, 1), :] = h[SUBS - 1 : SUBS, :]
        y_copies[g] = list(
            exchange(
                g, 0, ybuf.at[g, 0], lambda n, g=g: ybuf.at[g, n + 1], y_sem,
                [ctx_of(x, y + d, hi) for d in range(1, Y)],
            )
        )

    for g in range(GROUPS):
        direct = jnp.broadcast_to(sraw[g : g + 1, :], (SUBS, LANES))
        start = tuple(direct * gated[g, i] for i in range(STEP))

        def modes(block, acc):
            acc = list(acc)
            for rr in range(4):
                r = 4 * block + rr
                a = jnp.broadcast_to(rows[g, 0, pl.ds(r, 1), :], (SUBS, LANES))
                w = jnp.broadcast_to(rows[g, 1, pl.ds(r, 1), :], (SUBS, LANES))
                h = a * carry[g, r] + gated[g, 0]
                acc[0] = acc[0] + w * h
                for i in range(1, STEP):
                    h = h * a + gated[g, i]
                    acc[i] = acc[i] + w * h
            return tuple(acc)

        total = lax.fori_loop(0, MODES // 4, modes, start)
        for i in range(STEP):
            local[g, i] = total[i]

    before_rows = {}
    for g in range(GROUPS):
        for copy in y_copies[g]:
            copy.wait_recv()
        two = rows[g, 3]
        prefix = jnp.zeros((MODES, LANES), F32)
        total = jnp.zeros((MODES, LANES), F32)
        for yy in range(Y):
            part = ybuf[g, lax.rem(y - yy + Y, Y)]
            total = total * two + part
            prefix = jnp.where(yy < y, prefix * two + part, prefix)
        before_rows[g] = prefix
        xbuf[g, 0] = total
        x_copies[g] = list(
            exchange(
                g, 7, xbuf.at[g, 0], lambda n, g=g: xbuf.at[g, n + 1], x_sem,
                [ctx_of(x + d, y, hi) for d in range(1, X)],
            )
        )
    own = {}
    for g in range(GROUPS):
        for copy in x_copies[g]:
            copy.wait_recv()
        acc = jnp.zeros((MODES, LANES), F32)
        for xx in range(X):
            part = xbuf[g, lax.rem(x - xx + X, X)]
            acc = jnp.where(xx < x, acc * rows[g, 4] + part, acc)
        plane = before_rows[g] + rows[g, 5] * acc
        one, two = rows[g, 2], rows[g, 3]
        own[g] = one * plane
        zbuf[g, 0] = jnp.where(hi == 0, two * plane + ybuf[g, 0], plane)
        z_copies[g] = list(
            exchange(g, 10, zbuf.at[g, 0], lambda n, g=g: zbuf.at[g, 1], z_sem, [mate])
        )
    loads[6].wait()
    for g in range(GROUPS):
        z_copies[g][0].wait_recv()
        rows[g, 6] = own[g] + zbuf[g, 1]
        acc = [local[g, i] for i in range(STEP)]
        for r in range(MODES):
            a = jnp.broadcast_to(rows[g, 0, r : r + 1, :], (SUBS, LANES))
            w = jnp.broadcast_to(rows[g, 1, r : r + 1, :], (SUBS, LANES))
            state = jnp.broadcast_to(rows[g, 6, r : r + 1, :], (SUBS, LANES))
            q = (w * a) * (coef[g, r, 3] * state)
            acc[0] = acc[0] + q
            for i in range(1, STEP):
                q = q * a
                acc[i] = acc[i] + q
        for i in range(STEP):
            mixed[g, pl.ds(i, SUBS, stride=STEP), :] = acc[i]
        part = pl.ds(g * LANES, LANES)
        back = mixed[g].T.astype(BF16).astype(F32)
        out[part, :] = (qbuf[part, :].astype(F32) * back).astype(BF16)
    for copy in sends:
        copy.wait_send()


def local(streams, medium_taps, decay_rates, mode_weights, skip_gain):
    channels = streams.shape[1]
    anywhere = pl.BlockSpec(memory_space=pltpu.MemorySpace.HBM)
    vmem = pltpu.VMEM
    dma = pltpu.SemaphoreType.DMA
    return pl.pallas_call(
        kernel,
        out_shape=jax.ShapeDtypeStruct((channels, CHUNK), BF16),
        in_specs=[anywhere] * 5,
        out_specs=pl.BlockSpec(memory_space=pltpu.VMEM),
        scratch_shapes=[
            vmem((channels, CHUNK), BF16),
            vmem((channels, CHUNK), BF16),
            vmem((channels, CHUNK), BF16),
            vmem((channels, TAPS), F32),
            vmem((channels, MODES), F32),
            vmem((channels, MODES), F32),
            vmem((GROUPS, LANES), F32),
            vmem((GROUPS, LANES, CHUNK), BF16),
            vmem((GROUPS, 2 * CHUNK, LANES), F32),
            vmem((GROUPS, CHUNK, LANES), F32),
            vmem((GROUPS, TAPS, LANES), F32),
            vmem((GROUPS, MODES, 4, SUBS, LANES), F32),
            vmem((GROUPS, 7, MODES, LANES), F32),
            vmem((GROUPS, STEP, SUBS, LANES), F32),
            vmem((GROUPS, STEP, SUBS, LANES), F32),
            vmem((GROUPS, MODES, SUBS, LANES), F32),
            vmem((GROUPS, CHUNK, LANES), F32),
            vmem((GROUPS, Y, MODES, LANES), F32),
            vmem((GROUPS, X, MODES, LANES), F32),
            vmem((GROUPS, 2, MODES, LANES), F32),
            dma((7,)),
            dma((2 + GROUPS * 11,)),
            dma((GROUPS,)),
            dma((GROUPS, Y - 1)),
            dma((GROUPS, X - 1)),
            dma((GROUPS, 1)),
        ],
        name="gated_modal",
        compiler_params=pltpu.CompilerParams(collective_id=0, has_side_effects=True),
    )(streams, medium_taps, decay_rates, mode_weights, skip_gain.reshape(GROUPS, LANES))


def solution(mesh):
    placed = (P(None, "tp", "ctx"), P("tp", None), P("tp", None), P("tp", None), P("tp"))
    return jax.shard_map(
        local, mesh=mesh, in_specs=placed, out_specs=P("tp", "ctx"), check_vma=False
    )
```

profile of v0, /device:TPU:16, one launch (start us, length us, event | category | flops | bytes accessed | tf_op | source)
XLA Modules:
  0.0 53.2 jit_solution(4312332656289773173)
XLA Ops:
  0.0 0.0 copy-start
  0.0 1.5 %copy.6.rates = f32[256,16]{1,0:T(8,128)} copy(f32[256,16]{0,1:T(8,128)} %param.7) | data formatting | bytes 32768 | tf_op args[2]
  1.5 0.0 copy-done
  1.5 0.7 %copy.7.weights = f32[256,16]{1,0:T(8,128)} copy(f32[256,16]{0,1:T(8,128)S(1)} %copy-done) | data formatting | bytes 32768 | tf_op args[3]
  2.2 49.5 %gated_modal.1 = bf16[256,128]{1,0:T(8,128)(2,1)} custom-call(bf16[3,256,128]{2,1,0:T(8,128)(2,1)} %streams.1, f32[256,128]{1,0:T(8,128)} %taps.1, f32[256,16]{1,0:T(8,128)} %copy.6.rates, f32[256,16]{1,0:T(8,128)} %copy.7.weights, f32[2,128]{1,0:T(2,128)} %bitcast.1), custom_call_target="tpu_custom_call" | custom-call | tf_op jit(solution)/shard_map/gated_modal/pallas_call | solution.py:249
  51.7 1.5 %copy.9 = bf16[256,128]{1,0:T(8,128)(2,1)} copy(bf16[256,128]{1,0:T(8,128)(2,1)} %gated_modal.1) | data formatting | bytes 131072
Async XLA Ops:
  0.0 1.5 %copy-start = (f32[256,16]{0,1:T(8,128)S(1)}, f32[256,16]{0,1:T(8,128)}, u32[]{:S(2)}) copy-start(f32[256,16]{0,1:T(8,128)} %param.8) | copy-start | bytes 49156
where the time goes:
time: 53.4 us; the launch traced here: 53.2 us
  Pallas kernels  49.5 us (93%)
  local copies, waits for them, and re-layouts  3.71 us (7%)
    pallas_call x1, Pallas kernels, local(): pl.pallas_call(kernel, out_shape=jax.ShapeDtypeStruct((channels, CHUNK),...  49.5 us
    unnamed x5, local copies, waits for them, and re-layouts  3.71 us

commit v1 on v0

v1 whole, which is shorter than its diff:
```python
import jax
import jax.numpy as jnp
from jax import lax
from jax.experimental import pallas as pl
from jax.experimental.pallas import tpu as pltpu
from jax.sharding import PartitionSpec as P

MESH = pl.DeviceIdType.MESH
F32 = jnp.float32
BF16 = jnp.bfloat16
X, Y = 4, 8
LANES = 128
CHUNK = 128
TAPS = 128
MODES = 16
SUBS = 8
STEP = CHUNK // SUBS
TILES = CHUNK // SUBS
GROUPS = 2
EVEN, ODD, PAST = 0, 1, 2


def ctx_of(x, y, hi):
    return (lax.rem(x + X, X) * Y + lax.rem(y + Y, Y)) * 2 + hi


def remote(src, dst, send, recv, ctx):
    return pltpu.make_async_remote_copy(
        src_ref=src,
        dst_ref=dst,
        send_sem=send,
        recv_sem=recv,
        device_id=(ctx, lax.axis_index("tp")),
        device_id_type=MESH,
    )


def wide(row):
    return jnp.broadcast_to(row, (SUBS, LANES))


def kernel(
    streams, taps, rates, weights, skip, out,
    vbuf, kbuf, qbuf, traw, rates_t, weights_t, direct,
    raw, past, tokens, keys, medium, series, coef, rows, gated, local, carry, mixed,
    state, ybuf, xbuf, zbuf,
    in_sem, raw_send, raw_sem, past_send, past_sem, back_send,
    y_send, y_sem, x_send, x_sem, z_send, z_sem,
):
    ctx = lax.axis_index("ctx")
    tp = lax.axis_index("tp")
    x, y, hi = ctx // 16, (ctx // 2) % 8, ctx % 2
    mate = ctx + 1 - 2 * hi
    count = lax.axis_size("ctx")
    following = lax.rem(ctx + 2, count)
    previous = lax.rem(ctx + count - 2, count)
    row_devices = [ctx_of(x, y + d, hi) for d in range(1, Y)]
    column_devices = [ctx_of(x + d, y, hi) for d in range(1, X)]
    barrier = pltpu.get_barrier_semaphore()
    part = [pl.ds(g * LANES, LANES) for g in range(GROUPS)]

    def raw_copy(which, g):
        return remote(
            streams.at[2 - which, part[g], :], raw.at[which, g],
            raw_send.at[which, g], raw_sem.at[which, g], mate,
        )

    def forward_copy(g):
        return remote(raw.at[0, g], past.at[g], past_send.at[g], past_sem.at[g], following)

    def back_copy(g):
        return remote(streams.at[2, part[g], :], past.at[g], back_send.at[g], past_sem.at[g], mate)

    def y_copy(g, n):
        return remote(
            ybuf.at[g, 0], ybuf.at[g, n + 1], y_send.at[g, n], y_sem.at[g, n], row_devices[n]
        )

    def x_copy(g, n):
        return remote(
            xbuf.at[g, 0], xbuf.at[g, n + 1], x_send.at[g, n], x_sem.at[g, n], column_devices[n]
        )

    def z_copy(g):
        return remote(zbuf.at[g, 0], zbuf.at[g, 1], z_send.at[g], z_sem.at[g], mate)

    @pl.when(hi == 0)
    def _():
        pl.semaphore_signal(barrier, inc=1, device_id=(mate, tp), device_id_type=MESH)
        for p in [following, previous] + row_devices + column_devices:
            pl.semaphore_signal(barrier, inc=1, device_id=(p, tp), device_id_type=MESH)

    @pl.when(hi == 1)
    def _():
        pl.semaphore_wait(barrier, 1)
        for which in range(2):
            for g in range(GROUPS):
                raw_copy(which, g).start()

    loads = []
    for n, (src, dst) in enumerate(
        ((rates, rates_t), (weights, weights_t), (taps, traw), (streams.at[2], vbuf),
         (streams.at[1], kbuf), (skip, direct), (streams.at[0], qbuf))
    ):
        copy = pltpu.make_async_copy(src, dst, in_sem.at[n])
        copy.start()
        loads.append(copy)

    sub = lax.broadcasted_iota(jnp.int32, (SUBS, LANES), 0)
    subf = sub.astype(F32)
    yf = y.astype(F32)
    loads[0].wait()
    loads[1].wait()
    for g in range(GROUPS):
        rate = rates_t[:, part[g]]
        rows[g, 0] = jnp.exp(-rate)
        rows[g, 1] = weights_t[:, part[g]] * jnp.sqrt(2.0 * rate)
        rows[g, 2] = jnp.exp(-128.0 * rate)
        rows[g, 3] = jnp.exp(-256.0 * rate)
        rows[g, 4] = jnp.exp(-2048.0 * rate)
        rows[g, 5] = jnp.exp((-256.0 * yf) * rate)
        for r in range(MODES):
            lam = wide(rates_t[r : r + 1, part[g]])
            coef[g, r, 0] = jnp.where(sub >= 1, jnp.exp(-16.0 * lam), 0.0)
            coef[g, r, 1] = jnp.where(sub >= 2, jnp.exp(-32.0 * lam), 0.0)
            coef[g, r, 2] = jnp.where(sub >= 4, jnp.exp(-64.0 * lam), 0.0)
            coef[g, r, 3] = jnp.exp(-16.0 * subf * lam)
    for n in range(2, 7):
        loads[n].wait()
    zeros = jnp.zeros((SUBS, LANES), F32)

    def lay(which, g, block):
        tokens[which, g, pl.ds(0, SUBS), :] = zeros
        tokens[which, g, pl.ds(SUBS, CHUNK), :] = block.astype(F32).T
        tokens[which, g, pl.ds(SUBS + CHUNK, SUBS), :] = zeros

    for g in range(GROUPS):
        traw[part[g], :] = traw[part[g], :].T

    def within(which, g, acc):
        def body(b, acc):
            acc = list(acc)
            window = [
                tokens[which, g, pl.ds(SUBS + SUBS * q - b, SUBS), :] for q in range(TILES)
            ]
            for a in range(TILES):
                tap = wide(traw[pl.ds(g * TAPS + SUBS * a + b, 1), :])
                for p in range(a, TILES):
                    acc[p] = acc[p] + tap * window[p - a]
            return tuple(acc)

        return lax.fori_loop(0, SUBS, body, tuple(acc))

    def across(which, g, acc):
        def body(b, acc):
            acc = list(acc)
            window = [
                tokens[which, g, pl.ds(2 * SUBS + SUBS * q - b, SUBS), :] for q in range(TILES)
            ]
            for a in range(TILES):
                tap = wide(traw[pl.ds(g * TAPS + SUBS * a + b, 1), :])
                for p in range(a + 1):
                    acc[p] = acc[p] + tap * window[TILES - 1 + p - a]
            return tuple(acc)

        return lax.fori_loop(0, SUBS, body, tuple(acc))

    def keep(which, g, acc):
        for p in range(TILES):
            medium[which, g, p] = acc[p]

    def kept(which, g):
        return tuple(medium[which, g, p] for p in range(TILES))

    def ends(which, g, acc, mine):
        for p in range(TILES):
            key = keys[which, g, pl.ds(SUBS * p, SUBS), :]
            series[which, g, pl.ds(SUBS * p, SUBS), :] = (key * acc[p]).astype(BF16).astype(F32)
        gate = [series[which, g, pl.ds(i, SUBS, stride=STEP), :] for i in range(STEP)]
        if mine:
            for i in range(STEP):
                gated[g, i] = gate[i]
        for r in range(MODES):
            a = wide(rows[g, 0, r : r + 1, :])
            h = gate[0]
            for i in range(1, STEP):
                h = h * a + gate[i]
            h = h + coef[g, r, 0] * pltpu.roll(h, 1, 0)
            h = h + coef[g, r, 1] * pltpu.roll(h, 2, 0)
            h = h + coef[g, r, 2] * pltpu.roll(h, 4, 0)
            if mine:
                carry[g, r] = jnp.where(sub >= 1, pltpu.roll(h, 1, 0), 0.0)
            state[which, g, pl.ds(r, 1), :] = h[SUBS - 1 : SUBS, :]

    def respond(g):
        skipped = wide(direct[g : g + 1, :])
        start = tuple(skipped * gated[g, i] for i in range(STEP))

        def modes(block, acc):
            acc = list(acc)
            for rr in range(4):
                r = 4 * block + rr
                a = wide(rows[g, 0, pl.ds(r, 1), :])
                w = wide(rows[g, 1, pl.ds(r, 1), :])
                h = a * carry[g, r] + gated[g, 0]
                acc[0] = acc[0] + w * h
                for i in range(1, STEP):
                    h = h * a + gated[g, i]
                    acc[i] = acc[i] + w * h
            return tuple(acc)

        total = lax.fori_loop(0, MODES // 4, modes, start)
        for i in range(STEP):
            local[g, i] = total[i]

    def finish(g, held, n):
        acc = [local[g, i] for i in range(STEP)]
        for r in range(MODES):
            a = wide(rows[g, 0, r : r + 1, :])
            w = wide(rows[g, 1, r : r + 1, :])
            q = (w * a) * (coef[g, r, 3] * wide(held[g, n, r : r + 1, :]))
            acc[0] = acc[0] + q
            for i in range(1, STEP):
                q = q * a
                acc[i] = acc[i] + q
        for i in range(STEP):
            mixed[g, pl.ds(i, SUBS, stride=STEP), :] = acc[i]
        back = mixed[g].T.astype(BF16).astype(F32)
        out[part[g], :] = (qbuf[part[g], :].astype(F32) * back).astype(BF16)

    @pl.when(hi == 0)
    def _():
        for g in range(GROUPS):
            lay(EVEN, g, vbuf[part[g], :])
            keys[EVEN, g] = kbuf[part[g], :].astype(F32).T
            keep(EVEN, g, within(EVEN, g, (zeros,) * TILES))
            keep(ODD, g, across(EVEN, g, (zeros,) * TILES))
        pl.semaphore_wait(barrier, Y + X)
        for g in range(GROUPS):
            raw_copy(0, g).wait_recv()
            forward_copy(g).start()
        for g in range(GROUPS):
            back_copy(g).start()
        for g in range(GROUPS):
            lay(ODD, g, raw[0, g])
            keep(ODD, g, within(ODD, g, kept(ODD, g)))
        for g in range(GROUPS):
            raw_copy(1, g).wait_recv()
            keys[ODD, g] = raw[1, g].astype(F32).T
            ends(ODD, g, kept(ODD, g), False)
        for g in range(GROUPS):
            forward_copy(g).wait_recv()
            lay(PAST, g, jnp.where(ctx > 0, past[g].astype(F32), 0.0))
            ends(EVEN, g, across(PAST, g, kept(EVEN, g)), True)
            ybuf[g, 0] = rows[g, 2] * state[EVEN, g] + state[ODD, g]
            for n in range(Y - 1):
                y_copy(g, n).start()
        for g in range(GROUPS):
            respond(g)
        prefixes = []
        for g in range(GROUPS):
            for n in range(Y - 1):
                y_copy(g, n).wait_recv()
            two = rows[g, 3]
            prefix = jnp.zeros((MODES, LANES), F32)
            total = jnp.zeros((MODES, LANES), F32)
            for yy in range(Y):
                term = ybuf[g, lax.rem(y - yy + Y, Y)]
                total = total * two + term
                prefix = jnp.where(yy < y, prefix * two + term, prefix)
            prefixes.append(prefix)
            xbuf[g, 0] = total
            for n in range(X - 1):
                x_copy(g, n).start()
        for g in range(GROUPS):
            for n in range(X - 1):
                x_copy(g, n).wait_recv()
            acc = jnp.zeros((MODES, LANES), F32)
            for xx in range(X):
                term = xbuf[g, lax.rem(x - xx + X, X)]
                acc = jnp.where(xx < x, acc * rows[g, 4] + term, acc)
            plane = prefixes[g] + rows[g, 5] * acc
            zbuf[g, 1] = plane
            zbuf[g, 0] = rows[g, 2] * plane + state[EVEN, g]
            z_copy(g).start()
        for g in range(GROUPS):
            finish(g, zbuf, 1)
        for g in range(GROUPS):
            forward_copy(g).wait_send()
            back_copy(g).wait_send()
            for n in range(Y - 1):
                y_copy(g, n).wait_send()
            for n in range(X - 1):
                x_copy(g, n).wait_send()
            z_copy(g).wait_send()

    @pl.when(hi == 1)
    def _():
        for g in range(GROUPS):
            lay(ODD, g, vbuf[part[g], :])
            keys[ODD, g] = kbuf[part[g], :].astype(F32).T
            keep(ODD, g, within(ODD, g, (zeros,) * TILES))
        for g in range(GROUPS):
            back_copy(g).wait_recv()
            lay(EVEN, g, past[g])
            ends(ODD, g, across(EVEN, g, kept(ODD, g)), True)
            respond(g)
        for g in range(GROUPS):
            z_copy(g).wait_recv()
            finish(g, zbuf, 1)
        for which in range(2):
            for g in range(GROUPS):
                raw_copy(which, g).wait_send()


def local(streams, medium_taps, decay_rates, mode_weights, skip_gain):
    channels = streams.shape[1]
    hbm = pl.BlockSpec(memory_space=pltpu.MemorySpace.HBM)
    vmem = pltpu.VMEM
    dma = pltpu.SemaphoreType.DMA
    return pl.pallas_call(
        kernel,
        out_shape=jax.ShapeDtypeStruct((channels, CHUNK), BF16),
        in_specs=[hbm] * 5,
        out_specs=pl.BlockSpec(memory_space=pltpu.VMEM),
        scratch_shapes=[
            vmem((channels, CHUNK), BF16),
            vmem((channels, CHUNK), BF16),
            vmem((channels, CHUNK), BF16),
            vmem((channels, TAPS), F32),
            vmem((MODES, channels), F32),
            vmem((MODES, channels), F32),
            vmem((GROUPS, LANES), F32),
            vmem((2, GROUPS, LANES, CHUNK), BF16),
            vmem((GROUPS, LANES, CHUNK), BF16),
            vmem((3, GROUPS, CHUNK + 2 * SUBS, LANES), F32),
            vmem((2, GROUPS, CHUNK, LANES), F32),
            vmem((2, GROUPS, TILES, SUBS, LANES), F32),
            vmem((2, GROUPS, CHUNK, LANES), F32),
            vmem((GROUPS, MODES, 4, SUBS, LANES), F32),
            vmem((GROUPS, 6, MODES, LANES), F32),
            vmem((GROUPS, STEP, SUBS, LANES), F32),
            vmem((GROUPS, STEP, SUBS, LANES), F32),
            vmem((GROUPS, MODES, SUBS, LANES), F32),
            vmem((GROUPS, CHUNK, LANES), F32),
            vmem((2, GROUPS, MODES, LANES), F32),
            vmem((GROUPS, Y, MODES, LANES), F32),
            vmem((GROUPS, X, MODES, LANES), F32),
            vmem((GROUPS, 2, MODES, LANES), F32),
            dma((7,)),
            dma((2, GROUPS)),
            dma((2, GROUPS)),
            dma((GROUPS,)),
            dma((GROUPS,)),
            dma((GROUPS,)),
            dma((GROUPS, Y - 1)),
            dma((GROUPS, Y - 1)),
            dma((GROUPS, X - 1)),
            dma((GROUPS, X - 1)),
            dma((GROUPS,)),
            dma((GROUPS,)),
        ],
        name="gated_modal",
        compiler_params=pltpu.CompilerParams(collective_id=0, has_side_effects=True),
    )(
        streams,
        medium_taps,
        decay_rates.T,
        mode_weights.T,
        skip_gain.reshape(GROUPS, LANES),
    )


def solution(mesh):
    placed = (P(None, "tp", "ctx"), P("tp", None), P("tp", None), P("tp", None), P("tp"))
    return jax.shard_map(
        local, mesh=mesh, in_specs=placed, out_specs=P("tp", "ctx"), check_vma=False
    )
```

time: 53.4 us -> 49.6 us (0.929)
  the two profiles are of different devices: /device:TPU:16 before, /device:TPU:64 now
where the time goes in v1:
time: 49.6 us; the launch traced here: 49.4 us
  Pallas kernels  47.9 us (97%)
  local copies, waits for them, and re-layouts  1.47 us (3%)
    pallas_call x1, Pallas kernels, local(): pl.pallas_call(kernel, out_shape=jax.ShapeDtypeStruct((channels, CHUNK),...  47.9 us
    unnamed x1, local copies, waits for them, and re-layouts  1.47 us

profile of v1, /device:TPU:64, one launch (start us, length us, event | category | flops | bytes accessed | tf_op | source)
XLA Modules:
  0.0 49.4 jit_solution(10739110552056181865)
XLA Ops:
  0.0 47.9 %gated_modal.1 = bf16[256,128]{1,0:T(8,128)(2,1)} custom-call(bf16[3,256,128]{2,1,0:T(8,128)(2,1)} %streams.1, f32[256,128]{1,0:T(8,128)} %taps.1, f32[16,256]{1,0:T(8,128)} %bitcast.3, f32[16,256]{1,0:T(8,128)} %bitcast.4, f32[2,128]{1,0:T(2,128)} %bitcast.5), custom_call_target="tpu_custom_call" | custom-call | tf_op jit(solution)/shard_map/gated_modal/pallas_call | solution.py:321
  47.9 1.5 %copy.7 = bf16[256,128]{1,0:T(8,128)(2,1)} copy(bf16[256,128]{1,0:T(8,128)(2,1)} %gated_modal.1) | data formatting | bytes 131072

commit v2 on v1

--- a/solution.py
+++ b/solution.py
@@ -50,6 +50,8 @@
     ctx = lax.axis_index("ctx")
     tp = lax.axis_index("tp")
     x, y, hi = ctx // 16, (ctx // 2) % 8, ctx % 2
+    low = tp // 2
+    later = jnp.logical_or(low == 5, low == 7)
     mate = ctx + 1 - 2 * hi
     count = lax.axis_size("ctx")
     following = lax.rem(ctx + 2, count)
@@ -93,9 +95,12 @@
     @pl.when(hi == 1)
     def _():
         pl.semaphore_wait(barrier, 1)
-        for which in range(2):
-            for g in range(GROUPS):
-                raw_copy(which, g).start()
+
+        @pl.when(jnp.logical_not(later))
+        def _():
+            for which in range(2):
+                for g in range(GROUPS):
+                    raw_copy(which, g).start()
 
     loads = []
     for n, (src, dst) in enumerate(
@@ -245,13 +250,13 @@
             lay(ODD, g, raw[0, g])
             keep(ODD, g, within(ODD, g, kept(ODD, g)))
         for g in range(GROUPS):
+            forward_copy(g).wait_recv()
+            lay(PAST, g, jnp.where(ctx > 0, past[g].astype(F32), 0.0))
+            ends(EVEN, g, across(PAST, g, kept(EVEN, g)), True)
+        for g in range(GROUPS):
             raw_copy(1, g).wait_recv()
             keys[ODD, g] = raw[1, g].astype(F32).T
             ends(ODD, g, kept(ODD, g), False)
-        for g in range(GROUPS):
-            forward_copy(g).wait_recv()
-            lay(PAST, g, jnp.where(ctx > 0, past[g].astype(F32), 0.0))
-            ends(EVEN, g, across(PAST, g, kept(EVEN, g)), True)
             ybuf[g, 0] = rows[g, 2] * state[EVEN, g] + state[ODD, g]
             for n in range(Y - 1):
                 y_copy(g, n).start()
@@ -300,6 +305,13 @@
             lay(ODD, g, vbuf[part[g], :])
             keys[ODD, g] = kbuf[part[g], :].astype(F32).T
             keep(ODD, g, within(ODD, g, (zeros,) * TILES))
+
+        @pl.when(later)
+        def _():
+            for which in range(2):
+                for g in range(GROUPS):
+                    raw_copy(which, g).start()
+
         for g in range(GROUPS):
             back_copy(g).wait_recv()
             lay(EVEN, g, past[g])
@@ -320,7 +332,7 @@
     dma = pltpu.SemaphoreType.DMA
     return pl.pallas_call(
         kernel,
-        out_shape=jax.ShapeDtypeStruct((channels, CHUNK), BF16),
+        out_shape=pltpu.VMEM((channels, CHUNK), BF16),
         in_specs=[hbm] * 5,
         out_specs=pl.BlockSpec(memory_space=pltpu.VMEM),
         scratch_shapes=[

time: 49.6 us -> 42.8 us (0.86)
  Pallas kernels: 47.9 us -> 42 us
  local copies, waits for them, and re-layouts: 1.47 us -> 0.63 us
    pallas_call x1, Pallas kernels: 47.9 us -> 42 us  [local(): pl.pallas_call(kernel, out_shape=pltpu.VMEM((channels, CHUNK), BF16), in_...]
    unnamed x1, local copies, waits for them, and re-layouts: 1.47 us -> 0.63 us
where the time goes in v2:
time: 42.8 us; the launch traced here: 42.6 us
  Pallas kernels  42 us (98%)
  local copies, waits for them, and re-layouts  0.63 us (1%)
    pallas_call x1, Pallas kernels, local(): pl.pallas_call(kernel, out_shape=pltpu.VMEM((channels, CHUNK), BF16), in_...  42 us

profile of v2, /device:TPU:64, one launch (start us, length us, event | category | flops | bytes accessed | tf_op | source)
XLA Modules:
  0.0 42.6 jit_solution(14437808614929625227)
XLA Ops:
  0.0 42.0 %gated_modal.1 = bf16[256,128]{1,0:T(8,128)(2,1)S(1)} custom-call(bf16[3,256,128]{2,1,0:T(8,128)(2,1)} %streams.1, f32[256,128]{1,0:T(8,128)} %taps.1, f32[16,256]{1,0:T(8,128)} %bitcast.3, f32[16,256]{1,0:T(8,128)} %bitcast.4, f32[2,128]{1,0:T(2,128)} %bitcast.5), custom_call_target="tpu_custom_call" | custom-call | tf_op jit(solution)/shard_map/gated_modal/pallas_call | solution.py:333
  42.0 0.6 %copy.7 = bf16[256,128]{1,0:T(8,128)(2,1)} copy(bf16[256,128]{1,0:T(8,128)(2,1)S(1)} %gated_modal.1) | data formatting | bytes 131072

commit v3 on v2

--- a/solution.py
+++ b/solution.py
@@ -8,7 +8,7 @@
 MESH = pl.DeviceIdType.MESH
 F32 = jnp.float32
 BF16 = jnp.bfloat16
-X, Y = 4, 8
+PAIRS = 32
 LANES = 128
 CHUNK = 128
 TAPS = 128
@@ -20,10 +20,6 @@
 EVEN, ODD, PAST = 0, 1, 2
 
 
-def ctx_of(x, y, hi):
-    return (lax.rem(x + X, X) * Y + lax.rem(y + Y, Y)) * 2 + hi
-
-
 def remote(src, dst, send, recv, ctx):
     return pltpu.make_async_remote_copy(
         src_ref=src,
@@ -43,21 +39,18 @@
     streams, taps, rates, weights, skip, out,
     vbuf, kbuf, qbuf, traw, rates_t, weights_t, direct,
     raw, past, tokens, keys, medium, series, coef, rows, gated, local, carry, mixed,
-    state, ybuf, xbuf, zbuf,
+    state, sums, zbuf,
     in_sem, raw_send, raw_sem, past_send, past_sem, back_send,
-    y_send, y_sem, x_send, x_sem, z_send, z_sem,
+    sum_send, sum_sem, z_send, z_sem,
 ):
     ctx = lax.axis_index("ctx")
     tp = lax.axis_index("tp")
-    x, y, hi = ctx // 16, (ctx // 2) % 8, ctx % 2
+    pair, hi = ctx // 2, ctx % 2
     low = tp // 2
-    later = jnp.logical_or(low == 5, low == 7)
     mate = ctx + 1 - 2 * hi
-    count = lax.axis_size("ctx")
-    following = lax.rem(ctx + 2, count)
-    previous = lax.rem(ctx + count - 2, count)
-    row_devices = [ctx_of(x, y + d, hi) for d in range(1, Y)]
-    column_devices = [ctx_of(x + d, y, hi) for d in range(1, X)]
+    after = PAIRS - 1 - pair
+    soon = jnp.logical_and(low != 3, jnp.logical_and(low != 5, low != 7))
+    late = jnp.logical_or(low == 5, low == 7)
     barrier = pltpu.get_barrier_semaphore()
     part = [pl.ds(g * LANES, LANES) for g in range(GROUPS)]
 
@@ -68,20 +61,18 @@
         )
 
     def forward_copy(g):
-        return remote(raw.at[0, g], past.at[g], past_send.at[g], past_sem.at[g], following)
+        return remote(raw.at[0, g], past.at[g], past_send.at[g], past_sem.at[g], ctx + 2)
 
     def back_copy(g):
         return remote(streams.at[2, part[g], :], past.at[g], back_send.at[g], past_sem.at[g], mate)
 
-    def y_copy(g, n):
-        return remote(
-            ybuf.at[g, 0], ybuf.at[g, n + 1], y_send.at[g, n], y_sem.at[g, n], row_devices[n]
-        )
-
-    def x_copy(g, n):
-        return remote(
-            xbuf.at[g, 0], xbuf.at[g, n + 1], x_send.at[g, n], x_sem.at[g, n], column_devices[n]
-        )
+    def pair_copy(n):
+        return remote(sums.at[0], sums.at[n], sum_send.at[n], sum_sem.at[n], ctx + 2 * n)
+
+    def start_raw():
+        for which in range(2):
+            for g in range(GROUPS):
+                raw_copy(which, g).start()
 
     def z_copy(g):
         return remote(zbuf.at[g, 0], zbuf.at[g, 1], z_send.at[g], z_sem.at[g], mate)
@@ -89,18 +80,20 @@
     @pl.when(hi == 0)
     def _():
         pl.semaphore_signal(barrier, inc=1, device_id=(mate, tp), device_id_type=MESH)
-        for p in [following, previous] + row_devices + column_devices:
-            pl.semaphore_signal(barrier, inc=1, device_id=(p, tp), device_id_type=MESH)
+
+        @pl.loop(1, pair + 1)
+        def _(n):
+            pl.semaphore_signal(
+                barrier, inc=1, device_id=(ctx - 2 * n, tp), device_id_type=MESH
+            )
 
     @pl.when(hi == 1)
     def _():
         pl.semaphore_wait(barrier, 1)
 
-        @pl.when(jnp.logical_not(later))
+        @pl.when(soon)
         def _():
-            for which in range(2):
-                for g in range(GROUPS):
-                    raw_copy(which, g).start()
+            start_raw()
 
     loads = []
     for n, (src, dst) in enumerate(
@@ -113,7 +106,6 @@
 
     sub = lax.broadcasted_iota(jnp.int32, (SUBS, LANES), 0)
     subf = sub.astype(F32)
-    yf = y.astype(F32)
     loads[0].wait()
     loads[1].wait()
     for g in range(GROUPS):
@@ -122,14 +114,17 @@
         rows[g, 1] = weights_t[:, part[g]] * jnp.sqrt(2.0 * rate)
         rows[g, 2] = jnp.exp(-128.0 * rate)
         rows[g, 3] = jnp.exp(-256.0 * rate)
-        rows[g, 4] = jnp.exp(-2048.0 * rate)
-        rows[g, 5] = jnp.exp((-256.0 * yf) * rate)
         for r in range(MODES):
             lam = wide(rates_t[r : r + 1, part[g]])
             coef[g, r, 0] = jnp.where(sub >= 1, jnp.exp(-16.0 * lam), 0.0)
             coef[g, r, 1] = jnp.where(sub >= 2, jnp.exp(-32.0 * lam), 0.0)
             coef[g, r, 2] = jnp.where(sub >= 4, jnp.exp(-64.0 * lam), 0.0)
             coef[g, r, 3] = jnp.exp(-16.0 * subf * lam)
+
+    @pl.when(jnp.logical_and(hi == 1, low == 3))
+    def _():
+        start_raw()
+
     for n in range(2, 7):
         loads[n].wait()
     zeros = jnp.zeros((SUBS, LANES), F32)
@@ -240,64 +235,76 @@
             keys[EVEN, g] = kbuf[part[g], :].astype(F32).T
             keep(EVEN, g, within(EVEN, g, (zeros,) * TILES))
             keep(ODD, g, across(EVEN, g, (zeros,) * TILES))
-        pl.semaphore_wait(barrier, Y + X)
+
+        @pl.when(after > 0)
+        def _():
+            pl.semaphore_wait(barrier, after)
+
         for g in range(GROUPS):
             raw_copy(0, g).wait_recv()
-            forward_copy(g).start()
+
+            @pl.when(after > 0)
+            def _():
+                forward_copy(g).start()
+
         for g in range(GROUPS):
             back_copy(g).start()
         for g in range(GROUPS):
             lay(ODD, g, raw[0, g])
             keep(ODD, g, within(ODD, g, kept(ODD, g)))
         for g in range(GROUPS):
-            forward_copy(g).wait_recv()
-            lay(PAST, g, jnp.where(ctx > 0, past[g].astype(F32), 0.0))
+
+            @pl.when(pair > 0)
+            def _():
+                forward_copy(g).wait_recv()
+
+            @pl.when(pair == 0)
+            def _():
+                past[g] = jnp.zeros((LANES, CHUNK), BF16)
+
+            lay(PAST, g, past[g])
             ends(EVEN, g, across(PAST, g, kept(EVEN, g)), True)
         for g in range(GROUPS):
             raw_copy(1, g).wait_recv()
             keys[ODD, g] = raw[1, g].astype(F32).T
             ends(ODD, g, kept(ODD, g), False)
-            ybuf[g, 0] = rows[g, 2] * state[EVEN, g] + state[ODD, g]
-            for n in range(Y - 1):
-                y_copy(g, n).start()
+            sums[0, g] = (rows[g, 2] * state[EVEN, g] + state[ODD, g]).astype(BF16)
+
+        @pl.loop(1, after + 1)
+        def _(n):
+            pair_copy(n).start()
+
         for g in range(GROUPS):
             respond(g)
-        prefixes = []
-        for g in range(GROUPS):
-            for n in range(Y - 1):
-                y_copy(g, n).wait_recv()
-            two = rows[g, 3]
-            prefix = jnp.zeros((MODES, LANES), F32)
-            total = jnp.zeros((MODES, LANES), F32)
-            for yy in range(Y):
-                term = ybuf[g, lax.rem(y - yy + Y, Y)]
-                total = total * two + term
-                prefix = jnp.where(yy < y, prefix * two + term, prefix)
-            prefixes.append(prefix)
-            xbuf[g, 0] = total
-            for n in range(X - 1):
-                x_copy(g, n).start()
-        for g in range(GROUPS):
-            for n in range(X - 1):
-                x_copy(g, n).wait_recv()
-            acc = jnp.zeros((MODES, LANES), F32)
-            for xx in range(X):
-                term = xbuf[g, lax.rem(x - xx + X, X)]
-                acc = jnp.where(xx < x, acc * rows[g, 4] + term, acc)
-            plane = prefixes[g] + rows[g, 5] * acc
-            zbuf[g, 1] = plane
-            zbuf[g, 0] = rows[g, 2] * plane + state[EVEN, g]
+
+        @pl.loop(1, pair + 1)
+        def _(n):
+            pair_copy(n).wait_recv()
+
+        def older(k, acc):
+            term = sums[pair - k]
+            return tuple(acc[g] * rows[g, 3] + term[g].astype(F32) for g in range(GROUPS))
+
+        nothing = jnp.zeros((MODES, LANES), F32)
+        planes = lax.fori_loop(0, pair, older, (nothing,) * GROUPS)
+        for g in range(GROUPS):
+            zbuf[g, 1] = planes[g]
+            zbuf[g, 0] = rows[g, 2] * planes[g] + state[EVEN, g]
             z_copy(g).start()
         for g in range(GROUPS):
             finish(g, zbuf, 1)
         for g in range(GROUPS):
-            forward_copy(g).wait_send()
+
+            @pl.when(after > 0)
+            def _():
+                forward_copy(g).wait_send()
+
             back_copy(g).wait_send()
-            for n in range(Y - 1):
-                y_copy(g, n).wait_send()
-            for n in range(X - 1):
-                x_copy(g, n).wait_send()
             z_copy(g).wait_send()
+
+        @pl.loop(1, after + 1)
+        def _(n):
+            pair_copy(n).wait_send()
 
     @pl.when(hi == 1)
     def _():
@@ -306,11 +313,9 @@
             keys[ODD, g] = kbuf[part[g], :].astype(F32).T
             keep(ODD, g, within(ODD, g, (zeros,) * TILES))
 
-        @pl.when(later)
+        @pl.when(late)
         def _():
-            for which in range(2):
-                for g in range(GROUPS):
-                    raw_copy(which, g).start()
+            start_raw()
 
         for g in range(GROUPS):
             back_copy(g).wait_recv()
@@ -350,14 +355,13 @@
             vmem((2, GROUPS, TILES, SUBS, LANES), F32),
             vmem((2, GROUPS, CHUNK, LANES), F32),
             vmem((GROUPS, MODES, 4, SUBS, LANES), F32),
-            vmem((GROUPS, 6, MODES, LANES), F32),
+            vmem((GROUPS, 4, MODES, LANES), F32),
             vmem((GROUPS, STEP, SUBS, LANES), F32),
             vmem((GROUPS, STEP, SUBS, LANES), F32),
             vmem((GROUPS, MODES, SUBS, LANES), F32),
             vmem((GROUPS, CHUNK, LANES), F32),
             vmem((2, GROUPS, MODES, LANES), F32),
-            vmem((GROUPS, Y, MODES, LANES), F32),
-            vmem((GROUPS, X, MODES, LANES), F32),
+            vmem((PAIRS, GROUPS, MODES, LANES), BF16),
             vmem((GROUPS, 2, MODES, LANES), F32),
             dma((7,)),
             dma((2, GROUPS)),
@@ -365,10 +369,8 @@
             dma((GROUPS,)),
             dma((GROUPS,)),
             dma((GROUPS,)),
-            dma((GROUPS, Y - 1)),
-            dma((GROUPS, Y - 1)),
-            dma((GROUPS, X - 1)),
-            dma((GROUPS, X - 1)),
+            dma((PAIRS,)),
+            dma((PAIRS,)),
             dma((GROUPS,)),
             dma((GROUPS,)),
         ],

time: 42.8 us -> 40.3 us (0.942)
  the two profiles are of different devices: /device:TPU:64 before, /device:TPU:262 now
where the time goes in v3:
time: 40.3 us; the launch traced here: 40.1 us
  Pallas kernels  39.5 us (98%)
  local copies, waits for them, and re-layouts  0.63 us (2%)
    pallas_call x1, Pallas kernels, local(): pl.pallas_call(kernel, out_shape=pltpu.VMEM((channels, CHUNK), BF16), in_...  39.5 us

profile of v3, /device:TPU:262, one launch (start us, length us, event | category | flops | bytes accessed | tf_op | source)
XLA Modules:
  0.0 40.1 jit_solution(11139432506429163601)
XLA Ops:
  0.0 39.5 %gated_modal.1 = bf16[256,128]{1,0:T(8,128)(2,1)S(1)} custom-call(bf16[3,256,128]{2,1,0:T(8,128)(2,1)} %streams.1, f32[256,128]{1,0:T(8,128)} %taps.1, f32[16,256]{1,0:T(8,128)} %bitcast.3, f32[16,256]{1,0:T(8,128)} %bitcast.4, f32[2,128]{1,0:T(2,128)} %bitcast.5), custom_call_target="tpu_custom_call" | custom-call | tf_op jit(solution)/shard_map/gated_modal/pallas_call | solution.py:338
  39.5 0.6 %copy.7 = bf16[256,128]{1,0:T(8,128)(2,1)} copy(bf16[256,128]{1,0:T(8,128)(2,1)S(1)} %gated_modal.1) | data formatting | bytes 131072

commit v4 on v3

--- a/solution.py
+++ b/solution.py
@@ -9,6 +9,7 @@
 F32 = jnp.float32
 BF16 = jnp.bfloat16
 PAIRS = 32
+ROWS = 4
 LANES = 128
 CHUNK = 128
 TAPS = 128
@@ -74,8 +75,8 @@
             for g in range(GROUPS):
                 raw_copy(which, g).start()
 
-    def z_copy(g):
-        return remote(zbuf.at[g, 0], zbuf.at[g, 1], z_send.at[g], z_sem.at[g], mate)
+    def z_copy():
+        return remote(zbuf.at[0], zbuf.at[1], z_send, z_sem, mate)
 
     @pl.when(hi == 0)
     def _():
@@ -213,12 +214,12 @@
         for i in range(STEP):
             local[g, i] = total[i]
 
-    def finish(g, held, n):
+    def finish(g, held):
         acc = [local[g, i] for i in range(STEP)]
         for r in range(MODES):
             a = wide(rows[g, 0, r : r + 1, :])
             w = wide(rows[g, 1, r : r + 1, :])
-            q = (w * a) * (coef[g, r, 3] * wide(held[g, n, r : r + 1, :]))
+            q = (w * a) * (coef[g, r, 3] * wide(held[g, r : r + 1, :]))
             acc[0] = acc[0] + q
             for i in range(1, STEP):
                 q = q * a
@@ -270,9 +271,13 @@
             ends(ODD, g, kept(ODD, g), False)
             sums[0, g] = (rows[g, 2] * state[EVEN, g] + state[ODD, g]).astype(BF16)
 
-        @pl.loop(1, after + 1)
-        def _(n):
-            pair_copy(n).start()
+        @pl.loop(0, PAIRS)
+        def _(m):
+            target = lax.rem(m, ROWS) * (PAIRS // ROWS) + m // ROWS
+
+            @pl.when(target > pair)
+            def _():
+                pair_copy(target - pair).start()
 
         for g in range(GROUPS):
             respond(g)
@@ -288,11 +293,12 @@
         nothing = jnp.zeros((MODES, LANES), F32)
         planes = lax.fori_loop(0, pair, older, (nothing,) * GROUPS)
         for g in range(GROUPS):
-            zbuf[g, 1] = planes[g]
-            zbuf[g, 0] = rows[g, 2] * planes[g] + state[EVEN, g]
-            z_copy(g).start()
-        for g in range(GROUPS):
-            finish(g, zbuf, 1)
+            zbuf[0, g] = rows[g, 2] * planes[g] + state[EVEN, g]
+        z_copy().start()
+        for g in range(GROUPS):
+            zbuf[1, g] = planes[g]
+        for g in range(GROUPS):
+            finish(g, zbuf.at[1])
         for g in range(GROUPS):
 
             @pl.when(after > 0)
@@ -300,11 +306,12 @@
                 forward_copy(g).wait_send()
 
             back_copy(g).wait_send()
-            z_copy(g).wait_send()
 
         @pl.loop(1, after + 1)
         def _(n):
             pair_copy(n).wait_send()
+
+        z_copy().wait_send()
 
     @pl.when(hi == 1)
     def _():
@@ -322,9 +329,9 @@
             lay(EVEN, g, past[g])
             ends(ODD, g, across(EVEN, g, kept(ODD, g)), True)
             respond(g)
-        for g in range(GROUPS):
-            z_copy(g).wait_recv()
-            finish(g, zbuf, 1)
+        z_copy().wait_recv()
+        for g in range(GROUPS):
+            finish(g, zbuf.at[1])
         for which in range(2):
             for g in range(GROUPS):
                 raw_copy(which, g).wait_send()
@@ -362,7 +369,7 @@
             vmem((GROUPS, CHUNK, LANES), F32),
             vmem((2, GROUPS, MODES, LANES), F32),
             vmem((PAIRS, GROUPS, MODES, LANES), BF16),
-            vmem((GROUPS, 2, MODES, LANES), F32),
+            vmem((2, GROUPS, MODES, LANES), F32),
             dma((7,)),
             dma((2, GROUPS)),
             dma((2, GROUPS)),
@@ -371,8 +378,8 @@
             dma((GROUPS,)),
             dma((PAIRS,)),
             dma((PAIRS,)),
-            dma((GROUPS,)),
-            dma((GROUPS,)),
+            pltpu.SemaphoreType.DMA,
+            pltpu.SemaphoreType.DMA,
         ],
         name="gated_modal",
         compiler_params=pltpu.CompilerParams(collective_id=0, has_side_effects=True),

time: 40.3 us -> 38.9 us (0.965)
  the two profiles are of different devices: /device:TPU:262 before, /device:TPU:902 now
where the time goes in v4:
time: 38.9 us; the launch traced here: 38.7 us
  Pallas kernels  38.1 us (98%)
  local copies, waits for them, and re-layouts  0.63 us (2%)
    pallas_call x1, Pallas kernels, local(): pl.pallas_call(kernel, out_shape=pltpu.VMEM((channels, CHUNK), BF16), in_...  38.1 us

profile of v4, /device:TPU:902, one launch (start us, length us, event | category | flops | bytes accessed | tf_op | source)
XLA Modules:
  0.0 38.7 jit_solution(5253215066821765616)
XLA Ops:
  0.0 38.1 %gated_modal.1 = bf16[256,128]{1,0:T(8,128)(2,1)S(1)} custom-call(bf16[3,256,128]{2,1,0:T(8,128)(2,1)} %streams.1, f32[256,128]{1,0:T(8,128)} %taps.1, f32[16,256]{1,0:T(8,128)} %bitcast.3, f32[16,256]{1,0:T(8,128)} %bitcast.4, f32[2,128]{1,0:T(2,128)} %bitcast.5), custom_call_target="tpu_custom_call" | custom-call | tf_op jit(solution)/shard_map/gated_modal/pallas_call | solution.py:345
  38.1 0.6 %copy.7 = bf16[256,128]{1,0:T(8,128)(2,1)} copy(bf16[256,128]{1,0:T(8,128)(2,1)S(1)} %gated_modal.1) | data formatting | bytes 131072

commit v5 on v4

--- a/solution.py
+++ b/solution.py
@@ -254,26 +254,26 @@
             lay(ODD, g, raw[0, g])
             keep(ODD, g, within(ODD, g, kept(ODD, g)))
         for g in range(GROUPS):
-
-            @pl.when(pair > 0)
-            def _():
-                forward_copy(g).wait_recv()
-
-            @pl.when(pair == 0)
-            def _():
-                past[g] = jnp.zeros((LANES, CHUNK), BF16)
-
-            lay(PAST, g, past[g])
-            ends(EVEN, g, across(PAST, g, kept(EVEN, g)), True)
-        for g in range(GROUPS):
             raw_copy(1, g).wait_recv()
             keys[ODD, g] = raw[1, g].astype(F32).T
             ends(ODD, g, kept(ODD, g), False)
+        for g in range(GROUPS):
+
+            @pl.when(pair > 0)
+            def _():
+                forward_copy(g).wait_recv()
+
+            @pl.when(pair == 0)
+            def _():
+                past[g] = jnp.zeros((LANES, CHUNK), BF16)
+
+            lay(PAST, g, past[g])
+            ends(EVEN, g, across(PAST, g, kept(EVEN, g)), True)
             sums[0, g] = (rows[g, 2] * state[EVEN, g] + state[ODD, g]).astype(BF16)
 
         @pl.loop(0, PAIRS)
         def _(m):
-            target = lax.rem(m, ROWS) * (PAIRS // ROWS) + m // ROWS
+            target = (ROWS - 1 - lax.rem(m, ROWS)) * (PAIRS // ROWS) + m // ROWS
 
             @pl.when(target > pair)
             def _():

time: 38.9 us -> 38.1 us (0.979)
  the two profiles are of different devices: /device:TPU:902 before, /device:TPU:906 now
where the time goes in v5:
time: 38.1 us; the launch traced here: 37.9 us
  Pallas kernels  37.2 us (98%)
  local copies, waits for them, and re-layouts  0.63 us (2%)
    pallas_call x1, Pallas kernels, local(): pl.pallas_call(kernel, out_shape=pltpu.VMEM((channels, CHUNK), BF16), in_...  37.2 us

profile of v5, /device:TPU:906, one launch (start us, length us, event | category | flops | bytes accessed | tf_op | source)
XLA Modules:
  0.0 37.9 jit_solution(8812618833328404438)
XLA Ops:
  0.0 37.2 %gated_modal.1 = bf16[256,128]{1,0:T(8,128)(2,1)S(1)} custom-call(bf16[3,256,128]{2,1,0:T(8,128)(2,1)} %streams.1, f32[256,128]{1,0:T(8,128)} %taps.1, f32[16,256]{1,0:T(8,128)} %bitcast.3, f32[16,256]{1,0:T(8,128)} %bitcast.4, f32[2,128]{1,0:T(2,128)} %bitcast.5), custom_call_target="tpu_custom_call" | custom-call | tf_op jit(solution)/shard_map/gated_modal/pallas_call | solution.py:345
  37.3 0.6 %copy.7 = bf16[256,128]{1,0:T(8,128)(2,1)} copy(bf16[256,128]{1,0:T(8,128)(2,1)S(1)} %gated_modal.1) | data formatting | bytes 131072
